TPU v7x, 256 devices: a whole 4x4x8 slice. The times are simulated.
256 devices in a mesh: slab: 16 (over x_hi, y, core), batch: 16 (over x_lo, z).
Axes of the slice: x: 4 (x_hi: 2, x_lo: 2; x = x_hi * 2 + x_lo), y: 4, z: 8, core: 2. Of those that a mesh axis runs over, the one named last changes fastest.
Arguments:
- volumes: bfloat16 [256, 2, 16384], P('slab', None, 'batch'), may hold values from -6 to 6
- band_weights: bfloat16 [2, 1024, 32], P(None, 'slab'), may hold values from -1 to 1
- band_start: int32 [2, 1024], P(None, 'slab'), may hold values from 0 to 224
- images: bfloat16 [6144, 16384], P('batch'), may hold values from -7 to 7
- noise_precision: float32 [6144], P('batch'), may hold values from 0.005004883 to 0.050048828
- log_prior: float32 [2, 1024], P(None, 'slab'), may hold values from -4 to 4
Outputs:
- responsibilities: float32 [2, 1024, 6144], P(None, 'slab', 'batch')
- log_evidence: float32 [6144], P('batch')
- backprojection: float32 [256, 2, 16384], P('slab', None, 'batch')
All inputs are finite; a program needn't handle non-finite values.
Results may differ from a plain program's by a relative error of at most 0.0069.
Values may be sent and summed in bfloat16 or wider, within the bound.
A program may use at most 64 MiB of HBM per device.

v0:
```python
import jax
import jax.numpy as jnp
from jax import lax
from jax.sharding import PartitionSpec as P


def joined_along(pieces, dim):
    pieces = jnp.moveaxis(pieces, 0, dim)
    shape = pieces.shape
    return pieces.reshape(*shape[:dim], shape[dim] * shape[dim + 1], *shape[dim + 2 :])


def copy_for_each(x, axis):
    copies = jnp.broadcast_to(x, (lax.axis_size(axis), *x.shape))
    return lax.all_to_all(copies, axis, split_axis=0, concat_axis=0, tiled=True)


def collect(x, axis, dim):
    return joined_along(copy_for_each(x, axis), dim)


def gathered_once(x, axis):
    leaves = jax.tree.leaves(x)
    sequence = sorted(range(len(leaves)), key=lambda k: -leaves[k].size)
    width = (1, *leaves[sequence[0]].shape)[-1]
    lines = [
        jnp.pad(leaves[k].reshape(-1), (0, -leaves[k].size % width)).reshape(-1, width)
        for k in sequence
    ]
    both, at, found = (copy_for_each(jnp.concatenate(lines), axis), 0, {})
    for k, line in zip(sequence, lines):
        piece = both[:, at : at + len(line)].reshape(len(both), -1)
        found[k] = piece[:, : leaves[k].size].reshape(-1, *leaves[k].shape)
        at += len(line)
    numbers = iter(range(len(leaves)))
    return jax.tree.map(lambda _: found[next(numbers)], x)


def folded_in_pairs(pieces, combine):
    while len(jax.tree.leaves(pieces)[0]) > 1:
        pieces = jax.vmap(combine)(
            *(jax.tree.map(lambda part: part[side::2], pieces) for side in (0, 1))
        )
    return jax.tree.map(lambda part: part[0], pieces)


def joined_all(x, axis, combine):
    pieces = gathered_once(x, axis)
    return folded_in_pairs(pieces, combine)


def cut_along(x, dim, count):
    before, after = (x.shape[:dim], x.shape[dim + 1 :])
    return jnp.moveaxis(x.reshape(*before, count, -1, *after), dim, 0)


def sum_at_owner(x, axis, dim):
    pieces = cut_along(x, dim, lax.axis_size(axis))
    arrived = lax.all_to_all(pieces, axis, split_axis=0, concat_axis=0, tiled=True)
    return arrived.sum(axis=0)


def build_slice(band_weights, band_start, planes):
    offsets = planes[None, None, :] - band_start[:, :, None]
    taps = jnp.arange(band_weights.shape[2], dtype=jnp.int32)
    hits = offsets[..., None] == taps
    values = jnp.where(hits, band_weights.astype(jnp.float32)[:, :, None, :], jnp.float32(0.0))
    return jnp.sum(values, axis=-1)


def combine_scores(first, second):
    top_one, total_one = first
    top_two, total_two = second
    joined = jnp.maximum(top_one, top_two)
    return (joined, total_one * jnp.exp(top_one - joined) + total_two * jnp.exp(top_two - joined))


def local(volumes, band_weights, band_start, images, noise_precision, log_prior):
    plane_count, classes, block = volumes.shape
    all_planes = plane_count * lax.axis_size("slab")
    slice_own = build_slice(band_weights, band_start, jnp.arange(all_planes, dtype=jnp.int32))
    gathered = collect(volumes, "slab", 0)
    projection = jnp.einsum(
        "koz,zkp->okp", slice_own.astype(jnp.bfloat16), gathered, preferred_element_type=jnp.float32
    ).astype(jnp.bfloat16)
    piece = lax.all_gather(projection, "batch", axis=2, tiled=True)
    columns = images
    inner = jnp.einsum("okp,np->kon", piece, columns, preferred_element_type=jnp.float32)
    wide = piece.astype(jnp.float32)
    inner, energy = (inner, jnp.sum(wide * wide, axis=2))
    score = (
        noise_precision[None, None, :] * (inner - 0.5 * energy.T[:, :, None])
        + log_prior[:, :, None]
    )
    local_top = jnp.max(score, axis=(0, 1))
    local_total = jnp.sum(jnp.exp(score - local_top[None, None, :]), axis=(0, 1))
    top, total = joined_all((local_top, local_total), "slab", combine_scores)
    log_evidence = top + jnp.log(total)
    responsibilities = jnp.exp(score - log_evidence[None, None, :])
    weights = responsibilities.astype(jnp.bfloat16)
    columns = images
    image_sum = lax.psum_scatter(
        jnp.einsum("np,kon->pko", columns, weights, preferred_element_type=jnp.float32),
        "batch",
        scatter_dimension=0,
        tiled=True,
    )
    backprojection = sum_at_owner(
        jnp.einsum("koz,pko->zkp", slice_own, image_sum, precision=lax.Precision.HIGHEST), "slab", 0
    )
    return (responsibilities, log_evidence, backprojection)


def solution(mesh):
    in_specs = (
        P("slab", None, "batch"),
        P(None, "slab", None),
        P(None, "slab"),
        P("batch", None),
        P("batch"),
        P(None, "slab"),
    )
    out_specs = (P(None, "slab", "batch"), P("batch"), P("slab", None, "batch"))
    return jax.shard_map(local, mesh=mesh, in_specs=in_specs, out_specs=out_specs, check_vma=False)
```

profile of v0, /device:TPU:2, one launch (start us, length us, event | category | flops | bytes accessed | tf_op | source)
XLA Modules:
  0.0 287.0 jit_solution(14780554154317257893)
XLA Ops:
  7.2 0.9 copy.20
  8.0 1.1 broadcast_in_dim.18
  9.1 6.1 %all-to-all-start = ((bf16[16,16,2,1024]{3,1,2,0:T(8,128)(2,1)}), bf16[16,16,2,1024]{3,1,2,0:T(8,128)(2,1)S(1)}, u32[]{:S(2)}, u32[]{:S(2)}) async-start(bf16[16,16,2,1024]{3,1,2,0:T(8,128)(2,1)} %broadcast_in_dim.18), calls=%async_computation | async-start | bytes 2097152 | tf_op jit(solution)/shard_map/all_to_all | solution.py:15
  15.3 0.0 all-gather.2.cloned.1.call-start
  15.3 0.8 copy.19
  16.1 0.8 iota_subtract_fusion
  16.9 0.0 copy-start.3
  16.9 0.0 copy-start.4
  16.9 1.1 select_reduce_fusion
  18.0 15.3 %all-to-all-done = bf16[16,16,2,1024]{3,1,2,0:T(8,128)(2,1)S(1)} async-done(((bf16[16,16,2,1024]{3,1,2,0:T(8,128)(2,1)}), bf16[16,16,2,1024]{3,1,2,0:T(8,128)(2,1)S(1)}, u32[]{:S(2)}, u32[]{:S(2)}) %all-to-all-start) | async-done | bytes 1048608 | tf_op jit(solution)/shard_map/all_to_all | solution.py:15
  33.3 0.1 copy.21
  33.4 1.0 fusion.3
  34.4 0.0 all-gather.2.cloned.1.call-update
  34.4 0.0 reduce-scatter.2.cloned.1.call-start
  34.5 74.9 %all-gather.2.cloned.1.call-done = bf16[64,2,16384]{2,0,1:T(8,128)(2,1)} async-done(((bf16[64,2,1024]{2,0,1:T(8,128)(2,1)}), bf16[64,2,16384]{2,0,1:T(8,128)(2,1)}) %all-gather.2.cloned.1.call-update) | async-done | bytes 4194320 | tf_op jit(solution)/shard_map/all_gather | solution.py:86
  109.4 0.0 copy-start
  109.4 3.3 %multiply_reduce_fusion = f32[64,2]{0,1:T(2,128)S(1)} fusion(bf16[64,2,16384]{2,0,1:T(8,128)(2,1)} %all-gather.2.cloned.1.call-done), kind=kLoop, calls=%fused_computation.4 | loop fusion | flops 6291328 | bytes 4194816 | tf_op jit(solution)/shard_map/reduce_sum | solution.py:90
  112.7 0.0 copy-done.3
  112.7 0.0 copy-done.4
  112.7 0.1 copy-done
  112.8 8.4 %fusion.21 = (f32[384]{0:T(512)S(1)}, f32[2,64,384]{2,1,0:T(8,128)S(1)}) fusion(f32[2,64]{1,0:T(2,128)S(1)} %copy-done.4, f32[2,64]{1,0:T(2,128)S(1)} %multiply_bitcast_fusion, bf16[64,2,16384]{2,0,1:T(8,128)(2,1)S(1)} %copy-done, bf16[384,16384]{1,0:T(8,128)(2,1)} %param.9, f32[384]{0:T(512)S(1)} %copy-done.3), kind=kOutput, calls=%fused_computation.32 | convolution fusion | flops 1610808960 | bytes 16977920 | tf_op jit(solution)/shard_map/okp,np->kon/dot_general | solution.py:88
  121.2 0.1 exponential_reduce_fusion
  121.3 13.6 %all_to_all.15 = f32[16,2,384]{2,1,0:T(2,128)S(1)} all-to-all(f32[16,2,384]{2,1,0:T(2,128)S(1)} %broadcast_in_dim.19), channel_id=1, replica_groups=mesh['slab'=16,'batch'=16] {'slab'}, dimensions={0} | all-to-all | bytes 98304 | tf_op jit(solution)/shard_map/all_to_all | solution.py:15
  135.4 0.0 copy-start.2
  135.4 0.0 copy-start.1
  135.4 10.2 %convolution_bitcast_fusion = f32[16384,2,64]{0,2,1:T(8,128)} fusion(bf16[384,16384]{1,0:T(8,128)(2,1)} %param.9, f32[2,64,384]{2,1,0:T(8,128)S(1)} %subtract_exponential_fusion), kind=kOutput, calls=%fused_computation | convolution fusion | flops 1610661888 | bytes 21168128 | tf_op jit(solution)/shard_map/np,kon->pko/dot_general | solution.py:103
  145.6 0.0 copy-done.2
  145.6 0.0 copy-done.1
  145.7 0.0 reduce-scatter.2.cloned.1.call-update
  145.7 95.3 %reduce-scatter.2.cloned.1.call-done = f32[1024,2,64]{0,2,1:T(8,128)} async-done(((f32[16384,2,64]{0,2,1:T(8,128)}), f32[1024,2,64]{0,2,1:T(8,128)}) %reduce-scatter.2.cloned.1.call-update) | async-done | bytes 524304 | tf_op jit(solution)/shard_map/reduce_scatter | solution.py:102
  241.0 2.9 %fusion.22 = f32[2,1024,256]{1,2,0:T(8,128)S(1)} fusion(f32[1024,2,64]{0,2,1:T(8,128)} %reduce-scatter.2.cloned.1.call-done, f32[2,64,256]{2,1,0:T(8,128)S(1)} %select_reduce_fusion), kind=kOutput, calls=%fused_computation.33 | convolution fusion | flops 402653184 | bytes 2752512 | tf_op jit(solution)/shard_map/koz,pko->zkp/dot_general | solution.py:109
  243.8 0.2 copy.23
  244.1 35.2 %all_to_all.16 = f32[16,16,2,1024]{3,1,2,0:T(8,128)S(1)} all-to-all(f32[16,16,2,1024]{3,1,2,0:T(8,128)S(1)} %copy.23), channel_id=1, replica_groups=mesh['slab'=16,'batch'=16] {'slab'}, dimensions={0} | all-to-all | bytes 4194304 | tf_op jit(solution)/shard_map/all_to_all | solution.py:59
  279.3 0.1 reduce_sum.39
  279.4 0.8 copy.25
  (24 shorter events, 0.4 us)
Async XLA Ops:
  9.1 24.2 %all-to-all-start = ((bf16[16,16,2,1024]{3,1,2,0:T(8,128)(2,1)}), bf16[16,16,2,1024]{3,1,2,0:T(8,128)(2,1)S(1)}, u32[]{:S(2)}, u32[]{:S(2)}) async-start(bf16[16,16,2,1024]{3,1,2,0:T(8,128)(2,1)} %broadcast_in_dim.18), calls=%async_computation | async-start | bytes 2097152 | tf_op jit(solution)/shard_map/all_to_all | solution.py:15
  15.3 94.1 %all-gather.2.cloned.1.call-start = ((), (), s32[]{:S(2)}) async-start(), calls=%async_computation.4 | async-start | bytes 4456448 | tf_op jit(solution)/shard_map/all_gather | solution.py:86
  16.9 95.8 %copy-start.3 = (f32[384]{0:T(512)S(1)}, f32[384]{0:T(512)}, u32[]{:S(2)}) copy-start(f32[384]{0:T(512)} %param.10) | copy-start | bytes 4612
  16.9 95.8 %copy-start.4 = (f32[2,64]{1,0:T(2,128)S(1)}, f32[2,64]{1,0:T(2,128)}, u32[]{:S(2)}) copy-start(f32[2,64]{1,0:T(2,128)} %param.11) | copy-start | bytes 1540
  34.4 206.5 %reduce-scatter.2.cloned.1.call-start = ((), (), s32[]{:S(2)}) async-start(), calls=%async_computation.5 | async-start | bytes 8912896 | tf_op jit(solution)/shard_map/reduce_scatter | solution.py:102
  109.4 3.4 %copy-start = (bf16[64,2,16384]{2,0,1:T(8,128)(2,1)S(1)}, bf16[64,2,16384]{2,0,1:T(8,128)(2,1)}, u32[]{:S(2)}) copy-start(bf16[64,2,16384]{2,0,1:T(8,128)(2,1)} %all-gather.2.cloned.1.call-done) | copy-start | bytes 12582916
  135.4 10.3 %copy-start.2 = (f32[384]{0:T(512)}, f32[384]{0:T(512)S(1)}, u32[]{:S(2)}) copy-start(f32[384]{0:T(512)S(1)} %add_reduce_fusion) | copy-start | bytes 4612
  135.4 10.2 %copy-start.1 = (f32[2,64,384]{2,1,0:T(8,128)}, f32[2,64,384]{2,1,0:T(8,128)S(1)}, u32[]{:S(2)}) copy-start(f32[2,64,384]{2,1,0:T(8,128)S(1)} %subtract_exponential_fusion) | copy-start | bytes 589828
Sparse Core Ops, SparseCore 0:
  34.6 74.7 all-gather.1
  145.8 95.1 reduce-scatter.1
where the time goes:
time: 289 us; the launch traced here: 287 us
  waiting for transfers between devices  185 us (64%)
  blocking collectives  48.8 us (17%)
  matrix products  22.5 us (8%)
  between operations  14.2 us (5%)
  starting transfers between devices  6.22 us (2%)
  other arithmetic  5.44 us (2%)
  local copies, waits for them, and re-layouts  4.35 us (2%)
    reduce_scatter x1, waiting for transfers between devices, local(): lax.psum_scatter(jnp.einsum('np,kon->pko', columns, weights, preferred_el...  95.3 us
    all_gather x1, waiting for transfers between devices, local(): piece = lax.all_gather(projection, 'batch', axis=2, tiled=True)  74.9 us
    all_to_all x1, blocking collectives, sum_at_owner(): lax.all_to_all(pieces, axis, split_axis=0, concat_axis=0, tiled=True)  35.2 us
    all_to_all x1, waiting for transfers between devices, copy_for_each(): return lax.all_to_all(copies, axis, split_axis=0, concat_axis=0, tiled=True)  15.3 us
    all_to_all x1, blocking collectives, copy_for_each(): return lax.all_to_all(copies, axis, split_axis=0, concat_axis=0, tiled=True)  13.6 us
    dot_general x1, matrix products, local(): jnp.einsum('np,kon->pko', columns, weights, preferred_element_type=jnp.fl...  10.2 us
    dot_general x1, matrix products, local(): jnp.einsum('okp,np->kon', piece, columns, preferred_element_type=jnp.floa...  8.4 us
    all_to_all x1, starting transfers between devices, copy_for_each(): return lax.all_to_all(copies, axis, split_axis=0, concat_axis=0, tiled=True)  6.14 us
  transfers between devices with their start and end apart: 3, of which 3 were waited for; matrix products, arithmetic and copies ran while one was open for 1% of the time, Pallas kernels for 0%

commit v1 on v0

v1 whole, which is shorter than its diff:
```python
import functools

import jax
import jax.numpy as jnp
from jax import lax
from jax.experimental import pallas as pl
from jax.experimental.pallas import tpu as pltpu
from jax.sharding import PartitionSpec as P

F32, BF16 = jnp.float32, jnp.bfloat16
MESH = pl.DeviceIdType.MESH
SLABS, BATCHES, RING = 16, 16, 8
NT = (((1,), (1,)), ((), ()))
NN = (((1,), (0,)), ((), ()))


def dot(a, b, dims=NN):
    return lax.dot_general(a, b, dims, preferred_element_type=F32)


def in_three(x):
    first = x.astype(BF16).astype(F32)
    second = (x - first).astype(BF16).astype(F32)
    third = (x - first - second).astype(BF16).astype(F32)
    return first, second, third


def body(
    vol, pack, noise, images, resp_out, ev_out, back_out,
    img, vall, vslab, slices, acc, gout, gin, eout, ein, dout, din, noise_col,
    scores, rout, rin, wout, win, right_out, right_in, left_out, left_in, x_out, x_in,
    img_sem, vb_send, vb_recv, vs_send, vs_recv, sl_send, sl_recv, few_send, few_recv,
    red_send, red_recv,
):
    s, b = lax.axis_index("slab"), lax.axis_index("batch")
    xl, z = lax.div(b, RING), lax.rem(b, RING)
    rows, width = 32, 1024
    started = []

    def block(other, dz):
        return lax.rem(xl + other, 2) * RING + lax.rem(z + dz + RING, RING)

    def send(src, dst, to, send_sem, recv_sem):
        copy = pltpu.make_async_remote_copy(
            src_ref=src, dst_ref=dst, send_sem=send_sem, recv_sem=recv_sem,
            device_id=to, device_id_type=MESH,
        )
        copy.start()
        started.append(copy)

    def arrived(ref, send_sem, recv_sem):
        pltpu.make_async_remote_copy(
            src_ref=ref, dst_ref=ref, send_sem=send_sem, recv_sem=recv_sem,
            device_id=(s, b), device_id_type=MESH,
        ).wait_recv()

    order = [(0, 0), (1, 0)]
    for h in (1, 2, 3):
        order += [(0, -h), (0, h), (1, -h), (1, h)]
    order += [(0, 4), (1, 4)]

    def load(i):
        at = block(*order[i])
        return pltpu.make_async_copy(
            images.at[:, pl.ds(pl.multiple_of(at * width, width), width)],
            img.at[at], img_sem.at[i],
        )

    for i in range(16):
        load(i).start()

    barrier = pltpu.get_barrier_semaphore()
    for j in range(1, SLABS):
        pl.semaphore_signal(barrier, inc=1, device_id=(lax.rem(s + j, SLABS), b), device_id_type=MESH)
    for j in range(1, BATCHES):
        pl.semaphore_signal(barrier, inc=1, device_id=(s, lax.rem(b + j, BATCHES)), device_id_type=MESH)

    start = pack[:, 32:33]
    lane = lax.broadcasted_iota(jnp.int32, (128, 256), 1).astype(F32)
    offset = lane - start
    own = jnp.zeros((128, 256), F32)
    for t in range(32):
        own = jnp.where(offset == float(t), pack[:, t : t + 1], own)
    slices[s] = own.astype(BF16)
    vslab[:, pl.ds(pl.multiple_of(s * 16, 16), 16), :] = vol[...]
    prior_row = jnp.transpose(pack[...])[33:34, :]
    noise_col[...] = jnp.transpose(
        jnp.concatenate([noise[...], jnp.zeros((125, 128), F32)], axis=0)
    )

    pl.semaphore_wait(barrier, SLABS + BATCHES - 2)

    right = (s, block(0, 1))
    left = (s, block(0, -1))
    beside = (s, block(1, 0))
    twin_index = s + 1 - 2 * lax.rem(s, 2)
    twin = (twin_index, b)

    def ring(other, h, side):
        return (0 if side > 0 else 10) + 2 * h + other

    def forward(other, h, side, src):
        at = block(other, -h * side)
        dst = vall.at[at]
        if h == 3:
            half = pl.ds(0 if side > 0 else width // 2, width // 2)
            src, dst = src.at[:, :, half], dst.at[:, :, half]
        k = ring(other, h + 1, side)
        send(src, dst, right if side > 0 else left, vb_send.at[k], vb_recv.at[k])

    def take(other, h, side):
        at = block(other, -h * side)
        ref = vall.at[at]
        if h == 4:
            ref = ref.at[:, :, pl.ds(0 if side > 0 else width // 2, width // 2)]
        k = ring(other, h, side)
        arrived(ref, vb_send.at[k], vb_recv.at[k])

    forward(0, 0, 1, vol)
    forward(0, 0, -1, vol)
    send(vol, vall.at[b], beside, vb_send.at[0], vb_recv.at[0])

    def planes_of(index):
        return vslab.at[:, pl.ds(pl.multiple_of(index * 16, 16), 16), :]

    for j in range(1, 8):
        to = (lax.rem(s + 2 * j, SLABS), b)
        send(vol, planes_of(s), to, vs_send.at[j], vs_recv.at[j])
    send(vol, planes_of(s), twin, vs_send.at[8], vs_recv.at[8])
    for j in range(1, 8):
        to = (lax.rem(s + 2 * j, SLABS), b)
        send(slices.at[s], slices.at[s], to, sl_send.at[j], sl_recv.at[j])
    send(slices.at[s], slices.at[s], twin, sl_send.at[8], sl_recv.at[8])

    def multiply(i, ref):
        load(i).wait()
        part = dot(img[block(*order[i])], ref[...].reshape(rows, width), NT)
        if i == 0:
            acc[...] = part
        else:
            acc[...] += part

    multiply(0, vol)
    arrived(vall.at[block(1, 0)], vb_send.at[0], vb_recv.at[0])
    for side in (1, -1):
        forward(1, 0, side, vall.at[block(1, 0)])
    multiply(1, vall.at[block(1, 0)])

    def hop(h, first):
        i = first
        for other in (0, 1):
            for side in (1, -1):
                take(other, h, side)
                forward(other, h, side, vall.at[block(other, -h * side)])
            for side in (1, -1):
                multiply(i, vall.at[block(other, -h * side)])
                i += 1

    hop(1, 2)
    for j in range(1, 8):
        origin = lax.rem(s + SLABS - 2 * j, SLABS)
        arrived(planes_of(origin), vs_send.at[j], vs_recv.at[j])
        send(planes_of(origin), planes_of(origin), twin, vs_send.at[8 + j], vs_recv.at[8 + j])
    hop(2, 6)
    for j in range(1, 8):
        origin = lax.rem(s + SLABS - 2 * j, SLABS)
        arrived(slices.at[origin], sl_send.at[j], sl_recv.at[j])
        send(slices.at[origin], slices.at[origin], twin, sl_send.at[8 + j], sl_recv.at[8 + j])
    for j in range(8):
        origin = lax.rem(twin_index + SLABS - 2 * j, SLABS)
        arrived(planes_of(origin), vs_send.at[8 + j], vs_recv.at[8 + j])

    sums = []
    for k in range(2):
        projection = dot(slices[s, 64 * k : 64 * k + 64, :], vslab[k])
        sums.append(jnp.sum(projection * projection, axis=1, keepdims=True))
    energy = jnp.concatenate(sums, axis=0)
    energy = jnp.transpose(jnp.broadcast_to(energy, (128, 128)))[0:8, :]
    eout[...] = energy
    ein[b] = energy
    for j in range(1, BATCHES):
        to = (s, lax.rem(b + j, BATCHES))
        send(eout, ein.at[b], to, few_send.at[0], few_recv.at[0])

    hop(3, 10)

    arrived(ein.at[pl.ds(0, 15)], few_send.at[0], few_recv.at[0])
    energy = jnp.sum(ein[...], axis=0)
    line = lax.broadcasted_iota(jnp.int32, (8, 128), 0)
    energy = jnp.where(line == 1, prior_row, energy)
    dout[...] = energy
    din[s] = energy
    for j in range(1, SLABS):
        to = (lax.rem(s + j, SLABS), b)
        send(dout, din.at[s], to, few_send.at[1], few_recv.at[1])

    for other in (0, 1):
        for side in (1, -1):
            take(other, 4, side)
        multiply(14 + other, vall.at[block(other, 4)])

    packed = jnp.concatenate(
        [acc[0:128, :], acc[128:256, :], acc[256:384, :], jnp.zeros((128, 32), F32)], axis=1
    )
    gout[...] = packed.reshape(SLABS, 8, 128)
    gin[s] = gout[s]
    for j in range(1, SLABS):
        index = lax.rem(s + j, SLABS)
        send(gout.at[index], gin.at[s], (index, b), few_send.at[2], few_recv.at[2])

    for j in range(8):
        origin = lax.rem(twin_index + SLABS - 2 * j, SLABS)
        arrived(slices.at[origin], sl_send.at[8 + j], sl_recv.at[8 + j])
    arrived(din.at[pl.ds(0, 15)], few_send.at[1], few_recv.at[1])
    arrived(gin.at[pl.ds(0, 15)], few_send.at[2], few_recv.at[2])

    lane = lax.broadcasted_iota(jnp.int32, (8, 128), 1)
    slot = lax.div(lane, 16)
    stacked = []
    for k in range(2):
        groups = []
        for g in range(3):
            halves = []
            for half in range(2):
                tile = jnp.zeros((8, 128), F32)
                for i in range(8):
                    shift = (16 * i - 32 * g - 16 * k) % 128
                    piece = gin[8 * half + i]
                    piece = pltpu.roll(piece, shift, 1) if shift else piece
                    tile = jnp.where(slot == i, piece, tile)
                halves.append(tile)
            groups.append(jnp.concatenate(halves, axis=1))
        stacked += in_three(jnp.concatenate(groups, axis=0))
    stacked = jnp.concatenate(stacked, axis=0).astype(BF16)

    nz = jnp.concatenate(
        [noise_col[pl.ds(pl.multiple_of(s * 8, 8), 8), g : g + 1] for g in range(3)], axis=0
    )
    wide_lane = lax.broadcasted_iota(jnp.int32, (24, 256), 1)
    first_class = lax.rem(wide_lane, 128) < 64
    top = None
    for t in range(8):
        pair = slices[2 * t : 2 * t + 2].reshape(256, 256)
        both = dot(stacked, pair, NT)
        inner = jnp.where(
            first_class,
            both[0:24] + both[24:48] + both[48:72],
            both[72:96] + both[96:120] + both[120:144],
        )
        energy = jnp.concatenate([din[2 * t, 0:1, :], din[2 * t + 1, 0:1, :]], axis=1)
        prior = jnp.concatenate([din[2 * t, 1:2, :], din[2 * t + 1, 1:2, :]], axis=1)
        score = nz * (inner - 0.5 * energy) + prior
        scores[t] = score
        top = score if top is None else jnp.maximum(top, score)
    top = jnp.max(top, axis=1, keepdims=True)
    total = jnp.zeros((24, 256), F32)
    for t in range(8):
        total += jnp.exp(scores[t] - top)
    evidence = top + jnp.log(jnp.sum(total, axis=1, keepdims=True))
    spread = jnp.zeros((48, 256), F32)
    wide_evidence = jnp.broadcast_to(evidence, (24, 128))
    for t in range(8):
        posterior = jnp.exp(scores[t] - evidence)
        for side in range(2):
            rout[2 * t + side, 0:24, :] = posterior[:, 128 * side : 128 * side + 128]
            rout[2 * t + side, 24:48, :] = wide_evidence
        weight = jnp.concatenate(
            [jnp.where(first_class, posterior, 0.0), jnp.where(first_class, 0.0, posterior)], axis=0
        ).astype(BF16)
        spread += dot(weight, slices[2 * t : 2 * t + 2].reshape(256, 256))

    for i in range(SLABS):
        tile = jnp.zeros((8, 128), F32)
        for k in range(2):
            for g in range(3):
                at = 24 * k + 8 * g
                piece = spread[at : at + 8, 128 * (i // 8) : 128 * (i // 8) + 128]
                shift = (32 * g + 16 * k - 16 * (i % 8)) % 128
                piece = pltpu.roll(piece, shift, 1) if shift else piece
                tile = jnp.where(slot == 2 * g + k, piece, tile)
        wout[i] = tile
    win[s] = wout[s]
    for j in range(1, SLABS):
        index = lax.rem(s + j, SLABS)
        send(wout.at[index], win.at[s], (index, b), few_send.at[3], few_recv.at[3])
    rin[s] = rout[s]
    for j in range(1, SLABS):
        index = lax.rem(s + j, SLABS)
        send(rout.at[index], rin.at[s], (index, b), few_send.at[4], few_recv.at[4])

    arrived(win.at[pl.ds(0, 15)], few_send.at[3], few_recv.at[3])
    turned = jnp.transpose(win[...].reshape(128, 128))
    turned = jnp.concatenate([turned[0:32], turned[32:64], turned[64:96]], axis=1)
    high = turned.astype(BF16).astype(F32)
    low = turned - high
    planes = jnp.concatenate([high, low], axis=0).astype(BF16)

    def partial(other, dz):
        both = dot(planes, img[block(other, dz)])
        return both[0:rows] + both[rows : 2 * rows]

    half = width // 2
    for other in (0, 1):
        part = partial(other, 4).astype(BF16)
        for side, out, into, at in ((1, right_out, right_in, 0), (-1, left_out, left_in, half)):
            k = (0 if side > 0 else 8) + 2 * 3 + other
            out[other, 3, :, at : at + half] = part[:, at : at + half]
            cut = (slice(None), pl.ds(at, half))
            send(
                out.at[other, 3].at[cut], into.at[other, 3].at[cut],
                right if side > 0 else left, red_send.at[k], red_recv.at[k],
            )
    for h in (3, 2, 1):
        for other in (0, 1):
            for side, out, into, at in ((1, right_out, right_in, 0), (-1, left_out, left_in, half)):
                part = partial(other, side * h)
                k = (0 if side > 0 else 8) + 2 * h + other
                came = into.at[other, h]
                if h == 3:
                    came = came.at[:, pl.ds(at, half)]
                arrived(came, red_send.at[k], red_recv.at[k])
                if h == 3:
                    out[other, h - 1, :, :] = part.astype(BF16)
                    out[other, h - 1, :, at : at + half] = (
                        part[:, at : at + half] + came[...].astype(F32)
                    ).astype(BF16)
                else:
                    out[other, h - 1, :, :] = (part + came[...].astype(F32)).astype(BF16)
                k = (0 if side > 0 else 8) + 2 * (h - 1) + other
                send(
                    out.at[other, h - 1], into.at[other, h - 1],
                    right if side > 0 else left, red_send.at[k], red_recv.at[k],
                )

    arrived(rin.at[pl.ds(0, 15)], few_send.at[4], few_recv.at[4])
    for g in range(3):
        turned = rin[:, 8 * g : 8 * g + 8, :].reshape(128, 128)
        resp_out[:, 128 * g : 128 * g + 128] = jnp.transpose(turned)
        turned = rin[:, 24 + 8 * g : 32 + 8 * g, :].reshape(128, 128)
        ev_out[g : g + 1, :] = jnp.transpose(turned)[0:1, :]

    def last(other):
        part = partial(other, 0)
        for side, into in ((1, right_in), (-1, left_in)):
            k = (0 if side > 0 else 8) + other
            arrived(into.at[other, 0], red_send.at[k], red_recv.at[k])
            part += into[other, 0].astype(F32)
        return part

    x_out[...] = last(1).astype(BF16)
    send(x_out, x_in, beside, red_send.at[16], red_recv.at[16])
    mine = last(0)
    arrived(x_in, red_send.at[16], red_recv.at[16])
    back_out[...] = mine + x_in[...].astype(F32)

    for copy in started:
        copy.wait_send()


def local(volumes, band_weights, band_start, images, noise_precision, log_prior):
    planes, classes, width = volumes.shape
    owned = band_weights.shape[1]
    count, particles = classes * owned, images.shape[0]
    vol = jnp.swapaxes(volumes, 0, 1)
    pack = jnp.concatenate(
        [
            band_weights.reshape(count, -1).astype(F32),
            band_start.reshape(count, 1).astype(F32),
            log_prior.reshape(count, 1),
            jnp.zeros((count, 94), F32),
        ],
        axis=1,
    )
    vmem = pl.BlockSpec(memory_space=pltpu.VMEM)
    dma = pltpu.SemaphoreType.DMA
    few = (SLABS, 8, 128)
    responsibilities, log_evidence, back = pl.pallas_call(
        body,
        out_shape=(
            jax.ShapeDtypeStruct((count, particles), F32),
            jax.ShapeDtypeStruct((3, 128), F32),
            jax.ShapeDtypeStruct((classes * planes, width), F32),
        ),
        in_specs=[vmem, vmem, vmem, pl.BlockSpec(memory_space=pl.ANY)],
        out_specs=(vmem, vmem, vmem),
        scratch_shapes=[
            pltpu.VMEM((BATCHES, particles, width), BF16),
            pltpu.VMEM((BATCHES, classes, planes, width), BF16),
            pltpu.VMEM((classes, SLABS * planes, width), BF16),
            pltpu.VMEM((SLABS, count, SLABS * planes), BF16),
            pltpu.VMEM((particles, classes * planes), F32),
            pltpu.VMEM(few, F32),
            pltpu.VMEM(few, F32),
            pltpu.VMEM((8, 128), F32),
            pltpu.VMEM((BATCHES, 8, 128), F32),
            pltpu.VMEM((8, 128), F32),
            pltpu.VMEM(few, F32),
            pltpu.VMEM((128, 128), F32),
            pltpu.VMEM((8, 24, 256), F32),
            pltpu.VMEM((SLABS, 48, 128), F32),
            pltpu.VMEM((SLABS, 48, 128), F32),
            pltpu.VMEM(few, F32),
            pltpu.VMEM(few, F32),
            pltpu.VMEM((2, 4, 32, width), BF16),
            pltpu.VMEM((2, 4, 32, width), BF16),
            pltpu.VMEM((2, 4, 32, width), BF16),
            pltpu.VMEM((2, 4, 32, width), BF16),
            pltpu.VMEM((32, width), BF16),
            pltpu.VMEM((32, width), BF16),
            dma((16,)),
            dma((20,)), dma((20,)),
            dma((16,)), dma((16,)),
            dma((16,)), dma((16,)),
            dma((5,)), dma((5,)),
            dma((17,)), dma((17,)),
        ],
        compiler_params=pltpu.CompilerParams(
            collective_id=0, has_side_effects=True, vmem_limit_bytes=48 * 1024 * 1024
        ),
    )(vol, pack, noise_precision.reshape(3, 128), images)
    return (
        responsibilities.reshape(classes, owned, particles),
        log_evidence.reshape(particles),
        jnp.swapaxes(back.reshape(classes, planes, width), 0, 1),
    )


def solution(mesh):
    in_specs = (
        P("slab", None, "batch"),
        P(None, "slab", None),
        P(None, "slab"),
        P("batch", None),
        P("batch"),
        P(None, "slab"),
    )
    out_specs = (P(None, "slab", "batch"), P("batch"), P("slab", None, "batch"))
    return jax.shard_map(local, mesh=mesh, in_specs=in_specs, out_specs=out_specs, check_vma=False)
```

time: 289 us -> 71.9 us (0.25)
  waiting for transfers between devices: 185 us -> 0 us
  Pallas kernels: 0 us -> 64.4 us
  blocking collectives: 48.8 us -> 0 us
  matrix products: 22.5 us -> 0 us
  between operations: 14.2 us -> 0.69 us
  starting transfers between devices: 6.22 us -> 0 us
  other arithmetic: 5.44 us -> 0.78 us
    reduce_scatter x1 -> x0, waiting for transfers between devices: 95.3 us -> none  [local(): lax.psum_scatter(jnp.einsum('np,kon->pko', columns, weights, preferred_el...]
    all_gather x1 -> x0, waiting for transfers between devices: 74.9 us -> none  [local(): piece = lax.all_gather(projection, 'batch', axis=2, tiled=True)]
    pallas_call x0 -> x1, Pallas kernels: none -> 64.4 us  [local(): pl.pallas_call(body, out_shape=(jax.ShapeDtypeStruct((count, particles),...]
    all_to_all x2 -> x0, blocking collectives: 48.8 us -> none  [the longest x1 35.2 us: sum_at_owner(): lax.all_to_all(pieces, axis, split_axis=0, concat_axis=0, tiled=True)]
    dot_general x4 -> x0, matrix products: 22.5 us -> none  [the longest x1 10.2 us: local(): jnp.einsum('np,kon->pko', columns, weights, preferred_element_type=jnp.fl...]
    all_to_all x1 -> x0, waiting for transfers between devices: 15.3 us -> none  [copy_for_each(): return lax.all_to_all(copies, axis, split_axis=0, concat_axis=0, tiled=True)]
    all_to_all x1 -> x0, starting transfers between devices: 6.14 us -> none  [copy_for_each(): return lax.all_to_all(copies, axis, split_axis=0, concat_axis=0, tiled=True)]
    reduce_sum x4 -> x0, other arithmetic: 4.54 us -> none  [the longest x1 3.29 us: local(): inner, energy = (inner, jnp.sum(wide * wide, axis=2))]
  transfers between devices with their start and end apart: 3 -> 0, of which waited for: 3 -> 0; matrix products, arithmetic and copies ran while one was open for 1% -> 0% of each run, Pallas kernels for 0% -> 0%
where the time goes in v1:
time: 71.9 us; the launch traced here: 71.2 us
  Pallas kernels  64.4 us (90%)
  local copies, waits for them, and re-layouts  5.37 us (7%)
  other arithmetic  0.78 us (1%)
    pallas_call x1, Pallas kernels, local(): pl.pallas_call(body, out_shape=(jax.ShapeDtypeStruct((count, particles),...  64.4 us
    unnamed x5, local copies, waits for them, and re-layouts  2.79 us

profile of v1, /device:TPU:2, one launch (start us, length us, event | category | flops | bytes accessed | tf_op | source)
XLA Modules:
  0.0 71.2 jit_solution(9220493847747207957)
XLA Ops:
  0.6 0.1 pad.3.clone
  0.7 0.7 convert_element_type.22
  1.4 0.1 convert_element_type.25
  1.5 0.9 %copy.17 = bf16[16,2,1024]{2,0,1:T(8,128)(2,1)S(1)} copy(bf16[16,2,1024]{2,1,0:T(2,128)(2,1)} %param.6) | data formatting | bytes 131072 | tf_op args[0]
  2.4 0.8 %copy.10 = f32[2,64,32]{2,1,0:T(8,128)S(1)} copy(bf16[2,64,32]{1,2,0:T(8,128)(2,1)} %param.7) | data formatting | bytes 24576 | tf_op jit(solution)/shard_map/convert_element_type | solution.py:367
  3.2 0.8 %reshape.44 = f32[128,1]{1,0:T(8,128)S(1)} reshape(f32[2,64]{1,0:T(2,128)} %param.11) | data formatting | bytes 1024 | tf_op jit(solution)/shard_map/reshape | solution.py:369
  4.0 0.1 maximum_maximum_fusion.pack
  4.1 0.0 copy-start
  4.1 0.7 copy-done
  4.8 64.4 %shard_map.85 = (f32[128,384]{1,0:T(8,128)S(1)}, f32[3,128]{1,0:T(4,128)S(1)}, f32[32,1024]{1,0:T(8,128)S(1)}) custom-call(bf16[2,16,1024]{2,1,0:T(8,128)(2,1)S(1)} %bitcast.11, f32[128,128]{1,0:T(8,128)S(1)} %maximum_maximum_fusion.pack, f32[3,128]{1,0:T(4,128)S(1)} %bitcast.15, bf16[384,16384]{1,0:T(8,128)(2,1)} %images.1), custom_call_target="tpu_custom_call" | custom-call | tf_op jit(solution)/shard_map/pallas_call | solution.py:377
  69.2 0.8 %copy.16 = f32[2,16,1024]{2,0,1:T(2,128)} copy(f32[2,16,1024]{2,1,0:T(8,128)S(1)} %bitcast.13) | data formatting | bytes 262144 | tf_op jit(solution)/shard_map/reshape | solution.py:424
  70.0 0.7 copy.20
  70.6 0.6 copy.21
  (1 shorter events, 0.0 us)
Async XLA Ops:
  4.1 0.7 copy-start

commit v2 on v1

v2 whole, which is shorter than its diff:
```python
import functools

import jax
import jax.numpy as jnp
from jax import lax
from jax.experimental import pallas as pl
from jax.experimental.pallas import tpu as pltpu
from jax.sharding import PartitionSpec as P

F32, BF16 = jnp.float32, jnp.bfloat16
MESH = pl.DeviceIdType.MESH
SLABS, BATCHES, RING = 16, 16, 8
NT = (((1,), (1,)), ((), ()))
NN = (((1,), (0,)), ((), ()))


def dot(a, b, dims=NN):
    return lax.dot_general(a, b, dims, preferred_element_type=F32)


def in_three(x):
    first = x.astype(BF16).astype(F32)
    second = (x - first).astype(BF16).astype(F32)
    third = (x - first - second).astype(BF16).astype(F32)
    return first, second, third


def body(
    vol_in, bands, starts, priors, noise, images, resp_out, ev_out, back_out,
    img, vol, vall, vslab, tables, slices, acc, gout, gin, eout, ein, prep,
    scores, rout, rin, wout, win, red_out, red_in, hold,
    img_sem, vb_send, vb_recv, vs_send, vs_recv, sl_send, sl_recv, few_send, few_recv,
    red_send, red_recv,
):
    s, b = lax.axis_index("slab"), lax.axis_index("batch")
    xl, z = lax.div(b, RING), lax.rem(b, RING)
    rows, width = 32, 1024
    started = []

    def block(other, dz):
        return lax.rem(xl + other, 2) * RING + lax.rem(z + dz + RING, RING)

    def send(src, dst, to, send_sem, recv_sem):
        copy = pltpu.make_async_remote_copy(
            src_ref=src, dst_ref=dst, send_sem=send_sem, recv_sem=recv_sem,
            device_id=to, device_id_type=MESH,
        )
        copy.start()
        started.append(copy)

    def arrived(ref, send_sem, recv_sem):
        pltpu.make_async_remote_copy(
            src_ref=ref, dst_ref=ref, send_sem=send_sem, recv_sem=recv_sem,
            device_id=(s, b), device_id_type=MESH,
        ).wait_recv()

    order = [(0, 0), (1, 0), (0, -1), (0, 1), (0, -2), (0, 2), (1, -1), (1, 1), (0, -3), (0, 3)]
    order += [(1, -2), (1, 2), (0, 4), (1, -3), (1, 3), (1, 4)]

    def load(i):
        at = block(*order[i])
        return pltpu.make_async_copy(
            images.at[:, pl.ds(pl.multiple_of(at * width, width), width)],
            img.at[at], img_sem.at[i],
        )

    for i in range(16):
        load(i).start()

    barrier = pltpu.get_barrier_semaphore()
    for j in range(1, SLABS):
        pl.semaphore_signal(barrier, inc=1, device_id=(lax.rem(s + j, SLABS), b), device_id_type=MESH)
    for j in range(1, BATCHES):
        pl.semaphore_signal(barrier, inc=1, device_id=(s, lax.rem(b + j, BATCHES)), device_id_type=MESH)

    for k in range(2):
        vol[k] = vol_in[:, k, :]
    vslab[:, pl.ds(pl.multiple_of(s * 16, 16), 16), :] = vol[...]

    tables[s, 0:32, :] = jnp.concatenate([bands[0], bands[1]], axis=1).astype(F32)
    tables[s, 32:33, :] = jnp.concatenate([starts[0:1, :], starts[1:2, :]], axis=1).astype(F32)
    tables[s, 33:34, :] = jnp.concatenate([priors[0:1, :], priors[1:2, :]], axis=1)
    tables[s, 34:40, :] = jnp.zeros((6, 128), F32)

    plane = lax.broadcasted_iota(jnp.int32, (128, 128), 1).astype(F32)

    def build(index):
        table = jnp.concatenate([tables[index], jnp.zeros((88, 128), F32)], axis=0)
        moved = jnp.transpose(table)
        start = jnp.broadcast_to(moved[:, 32:33], (128, 128))
        rest = jnp.where(start >= 128.0, start - 128.0, start)
        for step in (64, 32, 16, 8, 4, 2, 1):
            hit = rest >= float(step)
            moved = jnp.where(hit, pltpu.roll(moved, step, 1), moved)
            rest = jnp.where(hit, rest - float(step), rest)
        parts = []
        for first in (0.0, 128.0):
            offset = plane + first - start
            inside = jnp.logical_and(offset >= 0.0, offset < 32.0)
            parts.append(jnp.where(inside, moved, 0.0))
        slices[index] = jnp.concatenate(parts, axis=1).astype(BF16)

    def multiply(other, dz, ref):
        i = order.index((other, dz))
        load(i).wait()
        part = dot(img[block(other, dz)], ref[...].reshape(rows, width), NT)
        if i == 0:
            acc[...] = part
        else:
            acc[...] += part

    pl.semaphore_wait(barrier, SLABS + BATCHES - 2)

    right = (s, block(0, 1))
    left = (s, block(0, -1))
    beside = (s, block(1, 0))
    twin_index = s + 1 - 2 * lax.rem(s, 2)
    twin = (twin_index, b)

    half = width // 2
    ends = {1: 0, -1: half}

    near = {1: right, -1: left}
    far = {1: (s, block(0, 2)), -1: (s, block(0, -2))}

    def along(h, side):
        return 2 * (h - 1) + (side < 0)

    def across(h, side):
        return 8 if h == 0 else 7 + 2 * h + (side < 0)

    def part_of(other, ref):
        return ref.at[pl.ds(0, 1)] if other else ref

    def push(other, h, side, near_by, src=None):
        dst = vall.at[block(other, -side * (h - (1 if near_by else 2)))]
        src = part_of(other, dst if src is None else src)
        dst = part_of(other, dst)
        if h == 4:
            cut = pl.ds(ends[side], half)
            src, dst = src.at[:, :, cut], dst.at[:, :, cut]
        k = 16 * other + along(h, side)
        send(src, dst, (near if near_by else far)[side], vb_send.at[k], vb_recv.at[k])

    def take(other, h, side):
        ref = part_of(other, vall.at[block(other, -h * side)])
        if h == 4:
            ref = ref.at[:, :, pl.ds(ends[side], half)]
        k = 16 * other + along(h, side)
        arrived(ref, vb_send.at[k], vb_recv.at[k])

    def cross(h, side, src=None):
        k = across(h, side)
        dst = vall.at[block(0, -h * side)]
        src = dst if src is None else src
        if h:
            src, dst = src.at[pl.ds(1, 1)], dst.at[pl.ds(1, 1)]
        send(src, dst, beside, vb_send.at[k], vb_recv.at[k])

    def take_across(h, side):
        k = across(h, side)
        ref = vall.at[block(1, -h * side)]
        if h:
            ref = ref.at[pl.ds(1, 1)]
        arrived(ref, vb_send.at[k], vb_recv.at[k])

    for side in (1, -1):
        push(0, 2, side, False, vol)
    cross(0, 1, vol)
    for side in (1, -1):
        push(0, 1, side, True, vol)

    def planes_of(index):
        return vslab.at[:, pl.ds(pl.multiple_of(index * 16, 16), 16), :]

    for j in range(1, 8):
        to = (lax.rem(s + 2 * j, SLABS), b)
        send(vol, planes_of(s), to, vs_send.at[j], vs_recv.at[j])
    send(vol, planes_of(s), twin, vs_send.at[8], vs_recv.at[8])
    for j in range(1, 8):
        to = (lax.rem(s + 2 * j, SLABS), b)
        send(tables.at[s], tables.at[s], to, sl_send.at[j], sl_recv.at[j])
    send(tables.at[s], tables.at[s], twin, sl_send.at[8], sl_recv.at[8])

    def relay(ref, j, sends, recvs):
        arrived(ref, sends.at[j], recvs.at[j])
        send(ref, ref, twin, sends.at[8 + j], recvs.at[8 + j])

    def origin_of(index, j):
        return lax.rem(index + SLABS - 2 * j, SLABS)

    for g in range(3):
        prep[g : g + 1, :] = noise[pl.ds(128 * g, 128)].reshape(1, 128)
    prep[3:128, :] = jnp.zeros((125, 128), F32)
    prep[...] = jnp.transpose(prep[...])
    vslab[:, pl.ds(pl.multiple_of(s * 16, 16), 16), :] = vol[...]
    multiply(0, 0, vol)
    build(s)

    def stored(other, dz):
        multiply(other, dz, vall.at[block(other, dz)])

    def relay_far(other):
        for side in (1, -1):
            take(other, 2, side)
            push(other, 4, side, False)
            push(other, 3, side, True)

    take_across(0, 1)
    for side in (1, -1):
        push(1, 2, side, False)
    for side in (1, -1):
        push(1, 1, side, True)
    relay_far(0)
    for side in (1, -1):
        take(0, 1, side)
        cross(1, side)
    for side in (1, -1):
        cross(2, side)
    stored(1, 0)
    for dz in (-1, 1, -2, 2):
        stored(0, dz)
    for j in range(1, 8):
        relay(planes_of(origin_of(s, j)), j, vs_send, vs_recv)
    relay_far(1)
    for side in (1, -1):
        take(0, 3, side)
        cross(3, side)
    for side in (1, -1):
        take(0, 4, side)
    cross(4, 1)
    for side in (1, -1):
        take(1, 1, side)
        take_across(1, side)
        stored(1, -side)
    for j in range(8):
        origin = origin_of(twin_index, j)
        arrived(planes_of(origin), vs_send.at[8 + j], vs_recv.at[8 + j])

    sums = []
    for k in range(2):
        projection = dot(slices[s, 64 * k : 64 * k + 64, :], vslab[k])
        sums.append(jnp.sum(projection * projection, axis=1, keepdims=True))
    energy = jnp.concatenate(sums, axis=0)
    energy = jnp.transpose(jnp.broadcast_to(energy, (128, 128)))[0:8, :]
    eout[...] = energy
    ein[b] = energy
    for j in range(1, BATCHES):
        to = (s, lax.rem(b + j, BATCHES))
        send(eout, ein.at[b], to, few_send.at[0], few_recv.at[0])

    for j in range(1, 8):
        relay(tables.at[origin_of(s, j)], j, sl_send, sl_recv)
    for side in (1, -1):
        stored(0, -3 * side)
        take_across(2, side)
        stored(1, -2 * side)
    stored(0, 4)
    for j in range(1, 8):
        build(origin_of(s, j))
    for side in (1, -1):
        take(1, 3, side)
        take_across(3, side)
        stored(1, -3 * side)
    for side in (1, -1):
        take(1, 4, side)
    take_across(4, 1)
    stored(1, 4)

    arrived(ein.at[pl.ds(0, 15)], few_send.at[0], few_recv.at[0])
    energy = jnp.sum(ein[...], axis=0)

    packed = jnp.concatenate(
        [acc[0:128, :], acc[128:256, :], acc[256:384, :], jnp.zeros((128, 32), F32)], axis=1
    )
    gout[:, 0:8, :] = packed.reshape(SLABS, 8, 128)
    for i in range(SLABS):
        gout[i, 8:16, :] = energy
    gin[s] = gout[s]
    for j in range(1, SLABS):
        index = lax.rem(s + j, SLABS)
        send(gout.at[index], gin.at[s], (index, b), few_send.at[2], few_recv.at[2])

    for j in range(8):
        origin = origin_of(twin_index, j)
        arrived(tables.at[origin], sl_send.at[8 + j], sl_recv.at[8 + j])
        build(origin)
    arrived(gin.at[pl.ds(0, 15)], few_send.at[2], few_recv.at[2])

    lane = lax.broadcasted_iota(jnp.int32, (8, 128), 1)
    slot = lax.div(lane, 16)
    stacked = []
    for k in range(2):
        groups = []
        for g in range(3):
            halves = []
            for upper in range(2):
                tile = jnp.zeros((8, 128), F32)
                for i in range(8):
                    shift = (16 * i - 32 * g - 16 * k) % 128
                    piece = gin[8 * upper + i, 0:8, :]
                    piece = pltpu.roll(piece, shift, 1) if shift else piece
                    tile = jnp.where(slot == i, piece, tile)
                halves.append(tile)
            groups.append(jnp.concatenate(halves, axis=1))
        stacked += in_three(jnp.concatenate(groups, axis=0))
    stacked = jnp.concatenate(stacked, axis=0).astype(BF16)

    nz = jnp.concatenate(
        [prep[pl.ds(pl.multiple_of(s * 8, 8), 8), g : g + 1] for g in range(3)], axis=0
    )
    wide_lane = lax.broadcasted_iota(jnp.int32, (24, 256), 1)
    first_class = lax.rem(wide_lane, 128) < 64
    for t in range(8):
        both = dot(stacked, slices[2 * t : 2 * t + 2].reshape(256, 256), NT)
        scores[t] = jnp.where(
            first_class,
            both[0:24] + both[24:48] + both[48:72],
            both[72:96] + both[96:120] + both[120:144],
        )
    top = None
    for t in range(8):
        energy = jnp.concatenate([gin[2 * t, 8:9, :], gin[2 * t + 1, 8:9, :]], axis=1)
        prior = jnp.concatenate([tables[2 * t, 33:34, :], tables[2 * t + 1, 33:34, :]], axis=1)
        score = nz * (scores[t] - 0.5 * energy) + prior
        scores[t] = score
        top = score if top is None else jnp.maximum(top, score)
    top = jnp.max(top, axis=1, keepdims=True)
    total = jnp.zeros((24, 256), F32)
    for t in range(8):
        total += jnp.exp(scores[t] - top)
    evidence = top + jnp.log(jnp.sum(total, axis=1, keepdims=True))
    spread = jnp.zeros((48, 256), F32)
    wide_evidence = jnp.broadcast_to(evidence, (24, 128))
    for t in range(8):
        posterior = jnp.exp(scores[t] - evidence)
        for side in range(2):
            rout[2 * t + side, 0:24, :] = posterior[:, 128 * side : 128 * side + 128]
            rout[2 * t + side, 24:48, :] = wide_evidence
        weight = jnp.concatenate(
            [jnp.where(first_class, posterior, 0.0), jnp.where(first_class, 0.0, posterior)], axis=0
        ).astype(BF16)
        spread += dot(weight, slices[2 * t : 2 * t + 2].reshape(256, 256))

    for i in range(SLABS):
        tile = jnp.zeros((8, 128), F32)
        for k in range(2):
            for g in range(3):
                at = 24 * k + 8 * g
                piece = spread[at : at + 8, 128 * (i // 8) : 128 * (i // 8) + 128]
                shift = (32 * g + 16 * k - 16 * (i % 8)) % 128
                piece = pltpu.roll(piece, shift, 1) if shift else piece
                tile = jnp.where(slot == 2 * g + k, piece, tile)
        wout[i] = tile
    win[s] = wout[s]
    for j in range(1, SLABS):
        index = lax.rem(s + j, SLABS)
        send(wout.at[index], win.at[s], (index, b), few_send.at[3], few_recv.at[3])
    arrived(win.at[pl.ds(0, 15)], few_send.at[3], few_recv.at[3])
    rin[s] = rout[s]
    for j in range(1, SLABS):
        index = lax.rem(s + j, SLABS)
        send(rout.at[index], rin.at[s], (index, b), few_send.at[4], few_recv.at[4])

    turned = jnp.transpose(win[...].reshape(128, 128))
    turned = jnp.concatenate([turned[0:32], turned[32:64], turned[64:96]], axis=1)
    high = turned.astype(BF16).astype(F32)
    low = turned - high
    planes = jnp.concatenate([high, low], axis=0).astype(BF16)

    def partial(other, dz):
        both = dot(planes, img[block(other, dz)])
        return both[0:rows] + both[rows : 2 * rows]

    def region(ref, other, h, side):
        ref = ref.at[16 * other + along(h, side)]
        rows_of = pl.ds(0, 16 if other else 32)
        return ref.at[rows_of, pl.ds(ends[side], half)] if h == 4 else ref.at[rows_of]

    def pass_on(value, other, h, side, near_by):
        k = 16 * other + along(h, side)
        out, into = region(red_out, other, h, side), region(red_in, other, h, side)
        if h == 4:
            value = value[:, ends[side] : ends[side] + half]
        out[...] = value.astype(BF16)
        send(out, into, (near if near_by else far)[side], red_send.at[k], red_recv.at[k])

    def pass_across(value, k, first):
        cut = pl.ds(first, 16)
        out, into = red_out.at[k].at[cut], red_in.at[k].at[cut]
        out[...] = value.astype(BF16)
        send(out, into, beside, red_send.at[k], red_recv.at[k])

    def received(k, ref):
        arrived(ref, red_send.at[k], red_recv.at[k])
        return ref[...].astype(F32)

    def came(other, h, side):
        return received(16 * other + along(h, side), region(red_in, other, h, side))

    def split(h, side):
        part = partial(1, h * side)
        pass_across(part[16:32], across(h, side), 16)
        return part[0:16]

    def joined(h, side):
        k = across(h, side)
        part = partial(0, h * side)
        extra = received(k, red_in.at[k].at[pl.ds(16, 16)])
        return jnp.concatenate([part[0:16], part[16:32] + extra], axis=0)

    def gathered(part, other, side):
        at = ends[side]
        here = part[:, at : at + half] + came(other, 4, side)
        there = part[:, half - at : width - at]
        part = jnp.concatenate([here, there] if side > 0 else [there, here], axis=1)
        return part + came(other, 3, side)

    part = split(4, 1)
    for side in (1, -1):
        pass_on(part, 1, 4, side, False)
    for side in (1, -1):
        pass_on(split(3, side), 1, 3, side, True)
    part = joined(4, 1)
    for side in (1, -1):
        pass_on(part, 0, 4, side, False)
    for side in (1, -1):
        hold[(1 - side) // 2] = split(2, side)
    for side in (1, -1):
        pass_on(joined(3, side), 0, 3, side, True)
    for side in (1, -1):
        pass_on(gathered(hold[(1 - side) // 2], 1, side), 1, 2, side, False)
    for side in (1, -1):
        pass_on(split(1, side), 1, 1, side, True)
    hold[2] = split(0, 1)
    for side in (1, -1):
        pass_on(gathered(joined(2, side), 0, side), 0, 2, side, False)
    for side in (1, -1):
        pass_on(joined(1, side), 0, 1, side, True)
    part = hold[2]
    for h in (1, 2):
        for side in (1, -1):
            part += came(1, h, side)
    pass_across(part, 24, 0)

    arrived(rin.at[pl.ds(0, 15)], few_send.at[4], few_recv.at[4])
    for g in range(3):
        turned = rin[:, 8 * g : 8 * g + 8, :].reshape(128, 128)
        resp_out[:, 128 * g : 128 * g + 128] = jnp.transpose(turned)
        turned = rin[:, 24 + 8 * g : 32 + 8 * g, :].reshape(128, 128)
        ev_out[g : g + 1, :] = jnp.transpose(turned)[0:1, :]

    part = joined(0, 1)
    for h in (1, 2):
        for side in (1, -1):
            part += came(0, h, side)
    extra = received(24, red_in.at[24].at[pl.ds(0, 16)])
    part = jnp.concatenate([part[0:16] + extra, part[16:32]], axis=0)
    for k in range(2):
        back_out[:, k, :] = part[16 * k : 16 * k + 16]

    for copy in started:
        copy.wait_send()


def local(volumes, band_weights, band_start, images, noise_precision, log_prior):
    planes, classes, width = volumes.shape
    owned = band_weights.shape[1]
    count, particles = classes * owned, images.shape[0]
    vmem = pl.BlockSpec(memory_space=pltpu.VMEM)
    dma = pltpu.SemaphoreType.DMA
    few = (SLABS, 8, 128)
    responsibilities, log_evidence, back = pl.pallas_call(
        body,
        out_shape=(
            jax.ShapeDtypeStruct((count, particles), F32),
            jax.ShapeDtypeStruct((3, 128), F32),
            jax.ShapeDtypeStruct((planes, classes, width), F32),
        ),
        in_specs=[vmem] * 5 + [pl.BlockSpec(memory_space=pl.ANY)],
        out_specs=(vmem, vmem, vmem),
        scratch_shapes=[
            pltpu.VMEM((BATCHES, particles, width), BF16),
            pltpu.VMEM((classes, planes, width), BF16),
            pltpu.VMEM((BATCHES, classes, planes, width), BF16),
            pltpu.VMEM((classes, SLABS * planes, width), BF16),
            pltpu.VMEM((SLABS, 40, 128), F32),
            pltpu.VMEM((SLABS, count, SLABS * planes), BF16),
            pltpu.VMEM((particles, classes * planes), F32),
            pltpu.VMEM((SLABS, 16, 128), F32),
            pltpu.VMEM((SLABS, 16, 128), F32),
            pltpu.VMEM((8, 128), F32),
            pltpu.VMEM((BATCHES, 8, 128), F32),
            pltpu.VMEM((128, 128), F32),
            pltpu.VMEM((8, 24, 256), F32),
            pltpu.VMEM((SLABS, 48, 128), F32),
            pltpu.VMEM((SLABS, 48, 128), F32),
            pltpu.VMEM(few, F32),
            pltpu.VMEM(few, F32),
            pltpu.VMEM((25, 32, width), BF16),
            pltpu.VMEM((25, 32, width), BF16),
            pltpu.VMEM((3, 16, width), F32),
            dma((16,)),
            dma((24,)), dma((24,)),
            dma((16,)), dma((16,)),
            dma((16,)), dma((16,)),
            dma((5,)), dma((5,)),
            dma((25,)), dma((25,)),
        ],
        compiler_params=pltpu.CompilerParams(
            collective_id=0, has_side_effects=True, vmem_limit_bytes=48 * 1024 * 1024
        ),
    )(volumes, jnp.swapaxes(band_weights, 1, 2), band_start, log_prior, noise_precision, images)
    return (
        responsibilities.reshape(classes, owned, particles),
        log_evidence.reshape(particles),
        back,
    )


def solution(mesh):
    in_specs = (
        P("slab", None, "batch"),
        P(None, "slab", None),
        P(None, "slab"),
        P("batch", None),
        P("batch"),
        P(None, "slab"),
    )
    out_specs = (P(None, "slab", "batch"), P("batch"), P("slab", None, "batch"))
    return jax.shard_map(local, mesh=mesh, in_specs=in_specs, out_specs=out_specs, check_vma=False)
```

time: 71.9 us -> 66.9 us (0.930)
  Pallas kernels: 64.4 us -> 60.1 us
  other arithmetic: 0.78 us -> 0 us
    pallas_call x1, Pallas kernels: 64.4 us -> 60.1 us  [local(): pl.pallas_call(body, out_shape=(jax.ShapeDtypeStruct((count, particles),...]
    unnamed x5 -> x13, local copies, waits for them, and re-layouts: 2.79 us -> 5.5 us
    reshape x2 -> x0, local copies, waits for them, and re-layouts: 1.57 us -> none  [the longest x1 0.81 us: local(): log_prior.reshape(count, 1)]
    convert_element_type x2 -> x0, local copies, waits for them, and re-layouts: 0.94 us -> none  [the longest x1 0.8 us: local(): band_weights.reshape(count, -1).astype(F32)]
where the time goes in v2:
time: 66.9 us; the launch traced here: 66.2 us
  Pallas kernels  60.1 us (90%)
  local copies, waits for them, and re-layouts  5.5 us (8%)
    pallas_call x1, Pallas kernels, local(): pl.pallas_call(body, out_shape=(jax.ShapeDtypeStruct((count, particles),...  60.1 us
    unnamed x13, local copies, waits for them, and re-layouts  5.5 us

profile of v2, /device:TPU:2, one launch (start us, length us, event | category | flops | bytes accessed | tf_op | source)
XLA Modules:
  0.0 66.2 jit_solution(4890269065980743323)
XLA Ops:
  0.6 0.0 copy-start
  0.6 0.8 %copy-done = bf16[16,2,1024]{2,1,0:T(2,128)(2,1)S(1)} copy-done((bf16[16,2,1024]{2,1,0:T(2,128)(2,1)S(1)}, bf16[16,2,1024]{2,1,0:T(2,128)(2,1)}, u32[]{:S(2)}) %copy-start) | copy-done | bytes 65560
  1.5 0.0 copy-start.1
  1.5 0.7 %copy-done.1 = bf16[2,64,32]{1,2,0:T(8,128)(2,1)S(1)} copy-done((bf16[2,64,32]{1,2,0:T(8,128)(2,1)S(1)}, bf16[2,64,32]{1,2,0:T(8,128)(2,1)}, u32[]{:S(2)}) %copy-start.1) | copy-done | bytes 8216
  2.2 0.0 copy-start.2
  2.2 0.7 %copy-done.2 = f32[384]{0:T(512)S(1)} copy-done((f32[384]{0:T(512)S(1)}, f32[384]{0:T(512)}, u32[]{:S(2)}) %copy-start.2) | copy-done | bytes 1560
  2.9 0.0 copy-start.3
  2.9 0.7 %copy-done.3 = s32[2,64]{1,0:T(2,128)S(1)} copy-done((s32[2,64]{1,0:T(2,128)S(1)}, s32[2,64]{1,0:T(2,128)}, u32[]{:S(2)}) %copy-start.3) | copy-done | bytes 536
  3.6 0.0 copy-start.4
  3.6 0.7 %copy-done.4 = f32[2,64]{1,0:T(2,128)S(1)} copy-done((f32[2,64]{1,0:T(2,128)S(1)}, f32[2,64]{1,0:T(2,128)}, u32[]{:S(2)}) %copy-start.4) | copy-done | bytes 536
  4.2 60.1 %shard_map.85 = (f32[128,384]{1,0:T(8,128)S(1)}, f32[3,128]{1,0:T(4,128)S(1)}, f32[16,2,1024]{2,1,0:T(2,128)S(1)}) custom-call(bf16[16,2,1024]{2,1,0:T(2,128)(2,1)S(1)} %copy-done, bf16[2,32,64]{2,1,0:T(8,128)(2,1)S(1)} %bitcast.4, s32[2,64]{1,0:T(2,128)S(1)} %copy-done.3, f32[2,64]{1,0:T(2,128)S(1)} %copy-done.4, f32[384]{0:T(512)S(1)} %copy-done.2, ...), custom_call_target="tpu_custom_call" | custom-call | tf_op jit(solution)/shard_map/pallas_call | solution.py:473
  64.3 0.7 %copy.12 = f32[2,64,384]{2,1,0:T(8,128)} copy(f32[2,64,384]{2,1,0:T(8,128)S(1)} %bitcast.3) | data formatting | bytes 393216
  65.0 0.6 copy.13
  65.6 0.7 copy.14
Async XLA Ops:
  0.6 0.8 %copy-start = (bf16[16,2,1024]{2,1,0:T(2,128)(2,1)S(1)}, bf16[16,2,1024]{2,1,0:T(2,128)(2,1)}, u32[]{:S(2)}) copy-start(bf16[16,2,1024]{2,1,0:T(2,128)(2,1)} %vol_in.1) | copy-start | bytes 196612
  1.5 0.7 %copy-start.1 = (bf16[2,64,32]{1,2,0:T(8,128)(2,1)S(1)}, bf16[2,64,32]{1,2,0:T(8,128)(2,1)}, u32[]{:S(2)}) copy-start(bf16[2,64,32]{1,2,0:T(8,128)(2,1)} %param.7) | copy-start | bytes 24580
  2.2 0.7 %copy-start.2 = (f32[384]{0:T(512)S(1)}, f32[384]{0:T(512)}, u32[]{:S(2)}) copy-start(f32[384]{0:T(512)} %noise.1) | copy-start | bytes 4612
  2.9 0.7 %copy-start.3 = (s32[2,64]{1,0:T(2,128)S(1)}, s32[2,64]{1,0:T(2,128)}, u32[]{:S(2)}) copy-start(s32[2,64]{1,0:T(2,128)} %starts.1) | copy-start | bytes 1540
  3.6 0.7 %copy-start.4 = (f32[2,64]{1,0:T(2,128)S(1)}, f32[2,64]{1,0:T(2,128)}, u32[]{:S(2)}) copy-start(f32[2,64]{1,0:T(2,128)} %priors.1) | copy-start | bytes 1540

commit v3 on v2

--- a/solution.py
+++ b/solution.py
@@ -70,9 +70,8 @@
     barrier = pltpu.get_barrier_semaphore()
     for j in range(1, SLABS):
         pl.semaphore_signal(barrier, inc=1, device_id=(lax.rem(s + j, SLABS), b), device_id_type=MESH)
-    for j in range(1, BATCHES):
-        pl.semaphore_signal(barrier, inc=1, device_id=(s, lax.rem(b + j, BATCHES)), device_id_type=MESH)
-
+    for other, dz in ((0, 1), (0, -1), (0, 2), (0, -2), (1, 0)):
+        pl.semaphore_signal(barrier, inc=1, device_id=(s, block(other, dz)), device_id_type=MESH)
     for k in range(2):
         vol[k] = vol_in[:, k, :]
     vslab[:, pl.ds(pl.multiple_of(s * 16, 16), 16), :] = vol[...]
@@ -109,7 +108,7 @@
         else:
             acc[...] += part
 
-    pl.semaphore_wait(barrier, SLABS + BATCHES - 2)
+    pl.semaphore_wait(barrier, SLABS + 4)
 
     right = (s, block(0, 1))
     left = (s, block(0, -1))
@@ -173,21 +172,29 @@
     def planes_of(index):
         return vslab.at[:, pl.ds(pl.multiple_of(index * 16, 16), 16), :]
 
-    for j in range(1, 8):
-        to = (lax.rem(s + 2 * j, SLABS), b)
-        send(vol, planes_of(s), to, vs_send.at[j], vs_recv.at[j])
-    send(vol, planes_of(s), twin, vs_send.at[8], vs_recv.at[8])
-    for j in range(1, 8):
-        to = (lax.rem(s + 2 * j, SLABS), b)
-        send(tables.at[s], tables.at[s], to, sl_send.at[j], sl_recv.at[j])
-    send(tables.at[s], tables.at[s], twin, sl_send.at[8], sl_recv.at[8])
+    def slab_of(index, opposite, steps):
+        half_x = lax.rem(lax.div(index, 8) + opposite, 2)
+        y = lax.rem(lax.div(lax.rem(index, 8), 2) + steps + 4, 4)
+        return 8 * half_x + 2 * y + lax.rem(index, 2)
+
+    def origin_of(index, j):
+        return slab_of(index, 1, 4 - j) if j >= 4 else slab_of(index, 0, -j)
+
+    def spread_own(src, dst, sends, recvs):
+        send(src, dst, (slab_of(s, 1, 0), b), sends.at[4], recvs.at[4])
+        for j in (1, 2, 3):
+            send(src, dst, (slab_of(s, 0, j), b), sends.at[j], recvs.at[j])
+        send(src, dst, twin, sends.at[8], recvs.at[8])
 
     def relay(ref, j, sends, recvs):
         arrived(ref, sends.at[j], recvs.at[j])
+        if j == 4:
+            for i in (1, 2, 3):
+                send(ref, ref, (slab_of(s, 0, i), b), sends.at[4 + i], recvs.at[4 + i])
         send(ref, ref, twin, sends.at[8 + j], recvs.at[8 + j])
 
-    def origin_of(index, j):
-        return lax.rem(index + SLABS - 2 * j, SLABS)
+    spread_own(vol, planes_of(s), vs_send, vs_recv)
+    spread_own(tables.at[s], tables.at[s], sl_send, sl_recv)
 
     for g in range(3):
         prep[g : g + 1, :] = noise[pl.ds(128 * g, 128)].reshape(1, 128)
@@ -217,10 +224,12 @@
         cross(1, side)
     for side in (1, -1):
         cross(2, side)
+    relay(planes_of(origin_of(s, 4)), 4, vs_send, vs_recv)
+    relay(tables.at[origin_of(s, 4)], 4, sl_send, sl_recv)
     stored(1, 0)
     for dz in (-1, 1, -2, 2):
         stored(0, dz)
-    for j in range(1, 8):
+    for j in (1, 2, 3, 5, 6, 7):
         relay(planes_of(origin_of(s, j)), j, vs_send, vs_recv)
     relay_far(1)
     for side in (1, -1):
@@ -243,13 +252,12 @@
         sums.append(jnp.sum(projection * projection, axis=1, keepdims=True))
     energy = jnp.concatenate(sums, axis=0)
     energy = jnp.transpose(jnp.broadcast_to(energy, (128, 128)))[0:8, :]
-    eout[...] = energy
-    ein[b] = energy
-    for j in range(1, BATCHES):
-        to = (s, lax.rem(b + j, BATCHES))
-        send(eout, ein.at[b], to, few_send.at[0], few_recv.at[0])
-
-    for j in range(1, 8):
+    eout[0] = energy
+    ein[z] = energy
+    for j in range(1, RING):
+        send(eout.at[0], ein.at[z], (s, block(0, j)), few_send.at[0], few_recv.at[0])
+
+    for j in (1, 2, 3, 5, 6, 7):
         relay(tables.at[origin_of(s, j)], j, sl_send, sl_recv)
     for side in (1, -1):
         stored(0, -3 * side)
@@ -258,6 +266,9 @@
     stored(0, 4)
     for j in range(1, 8):
         build(origin_of(s, j))
+    arrived(ein.at[pl.ds(0, RING - 1)], few_send.at[0], few_recv.at[0])
+    eout[1] = jnp.sum(ein[0:RING], axis=0)
+    send(eout.at[1], ein.at[RING], beside, few_send.at[1], few_recv.at[1])
     for side in (1, -1):
         take(1, 3, side)
         take_across(3, side)
@@ -266,9 +277,8 @@
         take(1, 4, side)
     take_across(4, 1)
     stored(1, 4)
-
-    arrived(ein.at[pl.ds(0, 15)], few_send.at[0], few_recv.at[0])
-    energy = jnp.sum(ein[...], axis=0)
+    arrived(ein.at[RING], few_send.at[1], few_recv.at[1])
+    energy = eout[1] + ein[RING]
 
     packed = jnp.concatenate(
         [acc[0:128, :], acc[128:256, :], acc[256:384, :], jnp.zeros((128, 32), F32)], axis=1
@@ -331,12 +341,15 @@
         total += jnp.exp(scores[t] - top)
     evidence = top + jnp.log(jnp.sum(total, axis=1, keepdims=True))
     spread = jnp.zeros((48, 256), F32)
-    wide_evidence = jnp.broadcast_to(evidence, (24, 128))
+    column = lax.broadcasted_iota(jnp.int32, (8, 128), 1)
+    tile = jnp.zeros((8, 128), F32)
+    for g in range(3):
+        tile = jnp.where(column == g, evidence[8 * g : 8 * g + 8], tile)
     for t in range(8):
         posterior = jnp.exp(scores[t] - evidence)
         for side in range(2):
             rout[2 * t + side, 0:24, :] = posterior[:, 128 * side : 128 * side + 128]
-            rout[2 * t + side, 24:48, :] = wide_evidence
+            rout[2 * t + side, 24:32, :] = tile
         weight = jnp.concatenate(
             [jnp.where(first_class, posterior, 0.0), jnp.where(first_class, 0.0, posterior)], axis=0
         ).astype(BF16)
@@ -357,11 +370,6 @@
         index = lax.rem(s + j, SLABS)
         send(wout.at[index], win.at[s], (index, b), few_send.at[3], few_recv.at[3])
     arrived(win.at[pl.ds(0, 15)], few_send.at[3], few_recv.at[3])
-    rin[s] = rout[s]
-    for j in range(1, SLABS):
-        index = lax.rem(s + j, SLABS)
-        send(rout.at[index], rin.at[s], (index, b), few_send.at[4], few_recv.at[4])
-
     turned = jnp.transpose(win[...].reshape(128, 128))
     turned = jnp.concatenate([turned[0:32], turned[32:64], turned[64:96]], axis=1)
     high = turned.astype(BF16).astype(F32)
@@ -433,6 +441,10 @@
     for side in (1, -1):
         pass_on(split(1, side), 1, 1, side, True)
     hold[2] = split(0, 1)
+    rin[s] = rout[s]
+    for j in range(1, SLABS):
+        index = lax.rem(s + j, SLABS)
+        send(rout.at[index], rin.at[s], (index, b), few_send.at[4], few_recv.at[4])
     for side in (1, -1):
         pass_on(gathered(joined(2, side), 0, side), 0, 2, side, False)
     for side in (1, -1):
@@ -447,8 +459,7 @@
     for g in range(3):
         turned = rin[:, 8 * g : 8 * g + 8, :].reshape(128, 128)
         resp_out[:, 128 * g : 128 * g + 128] = jnp.transpose(turned)
-        turned = rin[:, 24 + 8 * g : 32 + 8 * g, :].reshape(128, 128)
-        ev_out[g : g + 1, :] = jnp.transpose(turned)[0:1, :]
+    ev_out[...] = jnp.transpose(rin[:, 24:32, :].reshape(128, 128))[0:3, :]
 
     part = joined(0, 1)
     for h in (1, 2):
@@ -489,12 +500,12 @@
             pltpu.VMEM((particles, classes * planes), F32),
             pltpu.VMEM((SLABS, 16, 128), F32),
             pltpu.VMEM((SLABS, 16, 128), F32),
-            pltpu.VMEM((8, 128), F32),
-            pltpu.VMEM((BATCHES, 8, 128), F32),
+            pltpu.VMEM((2, 8, 128), F32),
+            pltpu.VMEM((RING + 1, 8, 128), F32),
             pltpu.VMEM((128, 128), F32),
             pltpu.VMEM((8, 24, 256), F32),
-            pltpu.VMEM((SLABS, 48, 128), F32),
-            pltpu.VMEM((SLABS, 48, 128), F32),
+            pltpu.VMEM((SLABS, 32, 128), F32),
+            pltpu.VMEM((SLABS, 32, 128), F32),
             pltpu.VMEM(few, F32),
             pltpu.VMEM(few, F32),
             pltpu.VMEM((25, 32, width), BF16),

time: 66.9 us -> 64.2 us (0.960)
  Pallas kernels: 60.1 us -> 57.8 us
    pallas_call x1, Pallas kernels: 60.1 us -> 57.8 us  [local(): pl.pallas_call(body, out_shape=(jax.ShapeDtypeStruct((count, particles),...]
where the time goes in v3:
time: 64.2 us; the launch traced here: 63.9 us
  Pallas kernels  57.8 us (90%)
  local copies, waits for them, and re-layouts  5.5 us (9%)
  between operations  0.65 us (1%)
    pallas_call x1, Pallas kernels, local(): pl.pallas_call(body, out_shape=(jax.ShapeDtypeStruct((count, particles),...  57.8 us
    unnamed x13, local copies, waits for them, and re-layouts  5.5 us

profile of v3, /device:TPU:2, one launch (start us, length us, event | category | flops | bytes accessed | tf_op | source)
XLA Modules:
  0.0 63.9 jit_solution(12632915379476010964)
XLA Ops:
  0.6 0.0 copy-start
  0.6 0.8 %copy-done = bf16[16,2,1024]{2,1,0:T(2,128)(2,1)S(1)} copy-done((bf16[16,2,1024]{2,1,0:T(2,128)(2,1)S(1)}, bf16[16,2,1024]{2,1,0:T(2,128)(2,1)}, u32[]{:S(2)}) %copy-start) | copy-done | bytes 65560
  1.5 0.0 copy-start.1
  1.5 0.7 %copy-done.1 = bf16[2,64,32]{1,2,0:T(8,128)(2,1)S(1)} copy-done((bf16[2,64,32]{1,2,0:T(8,128)(2,1)S(1)}, bf16[2,64,32]{1,2,0:T(8,128)(2,1)}, u32[]{:S(2)}) %copy-start.1) | copy-done | bytes 8216
  2.2 0.0 copy-start.2
  2.2 0.7 %copy-done.2 = f32[384]{0:T(512)S(1)} copy-done((f32[384]{0:T(512)S(1)}, f32[384]{0:T(512)}, u32[]{:S(2)}) %copy-start.2) | copy-done | bytes 1560
  2.9 0.0 copy-start.3
  2.9 0.7 %copy-done.3 = s32[2,64]{1,0:T(2,128)S(1)} copy-done((s32[2,64]{1,0:T(2,128)S(1)}, s32[2,64]{1,0:T(2,128)}, u32[]{:S(2)}) %copy-start.3) | copy-done | bytes 536
  3.6 0.0 copy-start.4
  3.6 0.7 %copy-done.4 = f32[2,64]{1,0:T(2,128)S(1)} copy-done((f32[2,64]{1,0:T(2,128)S(1)}, f32[2,64]{1,0:T(2,128)}, u32[]{:S(2)}) %copy-start.4) | copy-done | bytes 536
  4.2 57.8 %shard_map.85 = (f32[128,384]{1,0:T(8,128)S(1)}, f32[3,128]{1,0:T(4,128)S(1)}, f32[16,2,1024]{2,1,0:T(2,128)S(1)}) custom-call(bf16[16,2,1024]{2,1,0:T(2,128)(2,1)S(1)} %copy-done, bf16[2,32,64]{2,1,0:T(8,128)(2,1)S(1)} %bitcast.4, s32[2,64]{1,0:T(2,128)S(1)} %copy-done.3, f32[2,64]{1,0:T(2,128)S(1)} %copy-done.4, f32[384]{0:T(512)S(1)} %copy-done.2, ...), custom_call_target="tpu_custom_call" | custom-call | tf_op jit(solution)/shard_map/pallas_call | solution.py:484
  62.0 0.7 %copy.12 = f32[2,64,384]{2,1,0:T(8,128)} copy(f32[2,64,384]{2,1,0:T(8,128)S(1)} %bitcast.3) | data formatting | bytes 393216
  62.7 0.6 copy.13
  63.3 0.7 %copy.14 = f32[16,2,1024]{2,1,0:T(2,128)} copy(f32[16,2,1024]{2,1,0:T(2,128)S(1)} %get-tuple-element.14) | data formatting | bytes 262144
Async XLA Ops:
  0.6 0.8 %copy-start = (bf16[16,2,1024]{2,1,0:T(2,128)(2,1)S(1)}, bf16[16,2,1024]{2,1,0:T(2,128)(2,1)}, u32[]{:S(2)}) copy-start(bf16[16,2,1024]{2,1,0:T(2,128)(2,1)} %vol_in.1) | copy-start | bytes 196612
  1.5 0.7 %copy-start.1 = (bf16[2,64,32]{1,2,0:T(8,128)(2,1)S(1)}, bf16[2,64,32]{1,2,0:T(8,128)(2,1)}, u32[]{:S(2)}) copy-start(bf16[2,64,32]{1,2,0:T(8,128)(2,1)} %param.7) | copy-start | bytes 24580
  2.2 0.7 %copy-start.2 = (f32[384]{0:T(512)S(1)}, f32[384]{0:T(512)}, u32[]{:S(2)}) copy-start(f32[384]{0:T(512)} %noise.1) | copy-start | bytes 4612
  2.9 0.7 %copy-start.3 = (s32[2,64]{1,0:T(2,128)S(1)}, s32[2,64]{1,0:T(2,128)}, u32[]{:S(2)}) copy-start(s32[2,64]{1,0:T(2,128)} %starts.1) | copy-start | bytes 1540
  3.6 0.7 %copy-start.4 = (f32[2,64]{1,0:T(2,128)S(1)}, f32[2,64]{1,0:T(2,128)}, u32[]{:S(2)}) copy-start(f32[2,64]{1,0:T(2,128)} %priors.1) | copy-start | bytes 1540

commit v4 on v3

--- a/solution.py
+++ b/solution.py
@@ -26,8 +26,8 @@
 
 
 def body(
-    vol_in, bands, starts, priors, noise, images, resp_out, ev_out, back_out,
-    img, vol, vall, vslab, tables, slices, acc, gout, gin, eout, ein, prep,
+    vol_hbm, bands_hbm, starts_hbm, priors_hbm, noise_hbm, images, resp_out, ev_out, back_out,
+    vol_in, bands, starts, priors, noise, img, vol, vall, vslab, tables, slices, acc, gout, gin, eout, ein, prep,
     scores, rout, rin, wout, win, red_out, red_in, hold,
     img_sem, vb_send, vb_recv, vs_send, vs_recv, sl_send, sl_recv, few_send, few_recv,
     red_send, red_recv,
@@ -64,6 +64,17 @@
             img.at[at], img_sem.at[i],
         )
 
+    small = [
+        pltpu.make_async_copy(src, dst, img_sem.at[16 + i])
+        for i, (src, dst) in enumerate(
+            (
+                (vol_hbm, vol_in), (bands_hbm, bands), (starts_hbm, starts),
+                (priors_hbm, priors), (noise_hbm, noise),
+            )
+        )
+    ]
+    for copy in small:
+        copy.start()
     for i in range(16):
         load(i).start()
 
@@ -72,6 +83,8 @@
         pl.semaphore_signal(barrier, inc=1, device_id=(lax.rem(s + j, SLABS), b), device_id_type=MESH)
     for other, dz in ((0, 1), (0, -1), (0, 2), (0, -2), (1, 0)):
         pl.semaphore_signal(barrier, inc=1, device_id=(s, block(other, dz)), device_id_type=MESH)
+    for copy in small:
+        copy.wait()
     for k in range(2):
         vol[k] = vol_in[:, k, :]
     vslab[:, pl.ds(pl.multiple_of(s * 16, 16), 16), :] = vol[...]
@@ -488,9 +501,14 @@
             jax.ShapeDtypeStruct((3, 128), F32),
             jax.ShapeDtypeStruct((planes, classes, width), F32),
         ),
-        in_specs=[vmem] * 5 + [pl.BlockSpec(memory_space=pl.ANY)],
+        in_specs=[pl.BlockSpec(memory_space=pltpu.HBM)] * 6,
         out_specs=(vmem, vmem, vmem),
         scratch_shapes=[
+            pltpu.VMEM((planes, classes, width), BF16),
+            pltpu.VMEM((classes, 32, owned), BF16),
+            pltpu.VMEM((classes, owned), jnp.int32),
+            pltpu.VMEM((classes, owned), F32),
+            pltpu.VMEM((particles,), F32),
             pltpu.VMEM((BATCHES, particles, width), BF16),
             pltpu.VMEM((classes, planes, width), BF16),
             pltpu.VMEM((BATCHES, classes, planes, width), BF16),
@@ -511,7 +529,7 @@
             pltpu.VMEM((25, 32, width), BF16),
             pltpu.VMEM((25, 32, width), BF16),
             pltpu.VMEM((3, 16, width), F32),
-            dma((16,)),
+            dma((21,)),
             dma((24,)), dma((24,)),
             dma((16,)), dma((16,)),
             dma((16,)), dma((16,)),
@@ -521,7 +539,15 @@
         compiler_params=pltpu.CompilerParams(
             collective_id=0, has_side_effects=True, vmem_limit_bytes=48 * 1024 * 1024
         ),
-    )(volumes, jnp.swapaxes(band_weights, 1, 2), band_start, log_prior, noise_precision, images)
+    )(
+        *(
+            pltpu.with_memory_space_constraint(x, pltpu.MemorySpace.HBM)
+            for x in (
+                volumes, jnp.swapaxes(band_weights, 1, 2), band_start, log_prior,
+                noise_precision, images,
+            )
+        )
+    )
     return (
         responsibilities.reshape(classes, owned, particles),
         log_evidence.reshape(particles),

time: 64.2 us -> 60.7 us (0.945)
  local copies, waits for them, and re-layouts: 5.5 us -> 1.91 us
    unnamed x13 -> x3, local copies, waits for them, and re-layouts: 5.5 us -> 1.91 us
where the time goes in v4:
time: 60.7 us; the launch traced here: 60.6 us
  Pallas kernels  58 us (96%)
  local copies, waits for them, and re-layouts  1.91 us (3%)
  between operations  0.64 us (1%)
    pallas_call x1, Pallas kernels, local(): pl.pallas_call(body, out_shape=(jax.ShapeDtypeStruct((count, particles),...  58 us
    unnamed x3, local copies, waits for them, and re-layouts  1.91 us

profile of v4, /device:TPU:2, one launch (start us, length us, event | category | flops | bytes accessed | tf_op | source)
XLA Modules:
  0.0 60.6 jit_solution(4130251829555663165)
XLA Ops:
  0.6 58.0 %shard_map.85 = (f32[128,384]{1,0:T(8,128)S(1)}, f32[3,128]{1,0:T(4,128)S(1)}, f32[16,2,1024]{2,1,0:T(2,128)S(1)}) custom-call(bf16[16,2,1024]{2,1,0:T(2,128)(2,1)} %vol_hbm.1, bf16[2,32,64]{2,1,0:T(8,128)(2,1)} %bitcast.5, s32[2,64]{1,0:T(2,128)} %starts_hbm.1, f32[2,64]{1,0:T(2,128)} %priors_hbm.1, f32[384]{0:T(512)} %noise_hbm.1, bf16[384,16384]{1,0:T(8,128)(2,1)} %images.1), custom_call_target="tpu_custom_call" | custom-call | tf_op jit(solution)/shard_map/pallas_call | solution.py:497
  58.7 0.7 %copy.12 = f32[2,64,384]{2,1,0:T(8,128)} copy(f32[2,64,384]{2,1,0:T(8,128)S(1)} %bitcast.3) | data formatting | bytes 393216
  59.4 0.6 copy.13
  59.9 0.7 %copy.14 = f32[16,2,1024]{2,1,0:T(2,128)} copy(f32[16,2,1024]{2,1,0:T(2,128)S(1)} %get-tuple-element.14) | data formatting | bytes 262144

commit v5 on v4

--- a/solution.py
+++ b/solution.py
@@ -63,6 +63,19 @@
             images.at[:, pl.ds(pl.multiple_of(at * width, width), width)],
             img.at[at], img_sem.at[i],
         )
+
+    def slab_of(index, opposite, steps):
+        half_x = lax.rem(lax.div(index, 8) + opposite, 2)
+        y = lax.rem(lax.div(lax.rem(index, 8), 2) + steps + 4, 4)
+        return 8 * half_x + 2 * y + lax.rem(index, 2)
+
+    twin_index = s + 1 - 2 * lax.rem(s, 2)
+    barrier = pltpu.get_barrier_semaphore()
+    peers = [(s, block(other, dz)) for other, dz in ((0, 1), (0, -1), (0, 2), (0, -2), (1, 0))]
+    peers += [(slab_of(s, 0, j), b) for j in (1, 2, 3)]
+    peers += [(slab_of(s, 1, 0), b), (twin_index, b)]
+    for peer in peers:
+        pl.semaphore_signal(barrier, inc=1, device_id=peer, device_id_type=MESH)
 
     small = [
         pltpu.make_async_copy(src, dst, img_sem.at[16 + i])
@@ -78,11 +91,6 @@
     for i in range(16):
         load(i).start()
 
-    barrier = pltpu.get_barrier_semaphore()
-    for j in range(1, SLABS):
-        pl.semaphore_signal(barrier, inc=1, device_id=(lax.rem(s + j, SLABS), b), device_id_type=MESH)
-    for other, dz in ((0, 1), (0, -1), (0, 2), (0, -2), (1, 0)):
-        pl.semaphore_signal(barrier, inc=1, device_id=(s, block(other, dz)), device_id_type=MESH)
     for copy in small:
         copy.wait()
     for k in range(2):
@@ -121,7 +129,7 @@
         else:
             acc[...] += part
 
-    pl.semaphore_wait(barrier, SLABS + 4)
+    pl.semaphore_wait(barrier, 10)
 
     right = (s, block(0, 1))
     left = (s, block(0, -1))
@@ -184,11 +192,6 @@
 
     def planes_of(index):
         return vslab.at[:, pl.ds(pl.multiple_of(index * 16, 16), 16), :]
-
-    def slab_of(index, opposite, steps):
-        half_x = lax.rem(lax.div(index, 8) + opposite, 2)
-        y = lax.rem(lax.div(lax.rem(index, 8), 2) + steps + 4, 4)
-        return 8 * half_x + 2 * y + lax.rem(index, 2)
 
     def origin_of(index, j):
         return slab_of(index, 1, 4 - j) if j >= 4 else slab_of(index, 0, -j)

time: 60.7 us -> 59.1 us (0.974)
  Pallas kernels: 58 us -> 56.5 us
    pallas_call x1, Pallas kernels: 58 us -> 56.5 us  [local(): pl.pallas_call(body, out_shape=(jax.ShapeDtypeStruct((count, particles),...]
where the time goes in v5:
time: 59.1 us; the launch traced here: 59 us
  Pallas kernels  56.5 us (96%)
  local copies, waits for them, and re-layouts  1.91 us (3%)
  between operations  0.64 us (1%)
    pallas_call x1, Pallas kernels, local(): pl.pallas_call(body, out_shape=(jax.ShapeDtypeStruct((count, particles),...  56.5 us
    unnamed x3, local copies, waits for them, and re-layouts  1.91 us

profile of v5, /device:TPU:2, one launch (start us, length us, event | category | flops | bytes accessed | tf_op | source)
XLA Modules:
  0.0 59.0 jit_solution(17692549132205840532)
XLA Ops:
  0.6 56.5 %shard_map.85 = (f32[128,384]{1,0:T(8,128)S(1)}, f32[3,128]{1,0:T(4,128)S(1)}, f32[16,2,1024]{2,1,0:T(2,128)S(1)}) custom-call(bf16[16,2,1024]{2,1,0:T(2,128)(2,1)} %vol_hbm.1, bf16[2,32,64]{2,1,0:T(8,128)(2,1)} %bitcast.5, s32[2,64]{1,0:T(2,128)} %starts_hbm.1, f32[2,64]{1,0:T(2,128)} %priors_hbm.1, f32[384]{0:T(512)} %noise_hbm.1, bf16[384,16384]{1,0:T(8,128)(2,1)} %images.1), custom_call_target="tpu_custom_call" | custom-call | tf_op jit(solution)/shard_map/pallas_call | solution.py:500
  57.1 0.7 %copy.12 = f32[2,64,384]{2,1,0:T(8,128)} copy(f32[2,64,384]{2,1,0:T(8,128)S(1)} %bitcast.3) | data formatting | bytes 393216
  57.8 0.6 copy.13
  58.4 0.7 %copy.14 = f32[16,2,1024]{2,1,0:T(2,128)} copy(f32[16,2,1024]{2,1,0:T(2,128)S(1)} %get-tuple-element.14) | data formatting | bytes 262144
